TPU v7x, 128 devices: a whole 4x4x4 slice. The times are simulated.
128 devices in a mesh: row: 16 (over x, z), col: 8 (over y, core).
Axes of the slice: x: 4, y: 4, z: 4, core: 2. Of those that a mesh axis runs over, the one named last changes fastest.
Arguments:
- features: float32 [136, 16384], P(None, 'row'), may hold values from -6 to 6
- factor: float32 [16384, 32768], P('row', 'col')
Outputs:
- panel: float32 [16384, 512], P(('row', 'col'))
All inputs are finite; a program needn't handle non-finite values.
Results may differ from a plain program's by a relative error of at most 0.000067.
Values sent between devices are 32-bit elements; how exact they have to be, the bound alone decides.
A program may use at most 128 MiB of HBM per device.

v0:
```python
import functools

import jax
import jax.numpy as jnp
from jax import lax
from jax.experimental import pallas as pl
from jax.experimental.pallas import tpu as pltpu
from jax.sharding import PartitionSpec as P

MESH = pl.DeviceIdType.MESH
HIGHEST = lax.Precision.HIGHEST
F32, BF16 = jnp.float32, jnp.bfloat16

B = 512
FEAT = 136
RIDGE = 40.0
TILE = 128
STRIP = 16
ROWS = 1024
SLAB = 512
SLABS = 8
PIECES = 32
SUB = 32
SKEW = 3
DEPTH = 5
ITEMS = 1 + PIECES + 4
SLOTS = ITEMS + SKEW * DEPTH

TREES = (
    (1, 48, 64, 48, 27, 39, 53, 36, 41, 49, 65, 49, 48, 64, 80, 64),
    (2, 23, 35, 48, 48, 40, 50, 64, 64, 58, 66, 80, 48, 46, 50, 64),
    (4, 48, 64, 48, 48, 64, 80, 64, 38, 52, 68, 52, 30, 33, 53, 45),
    (8, 48, 44, 29, 48, 64, 56, 43, 64, 80, 72, 58, 48, 64, 56, 34),
)
BLOCKS = [(i, j) for j in range(4) for i in range(j, 4)]
PLACE = {b: n for n, b in enumerate(BLOCKS)}
COLUMN = [PLACE[j, j] * TILE for j in range(4)]
SHARE = len(BLOCKS) * TILE // 8


def pick(index, table):
    value = jnp.int32(0)
    for n, entry in enumerate(table):
        value = value + jnp.where(index == n, jnp.int32(entry), jnp.int32(0))
    return value


def nt(a, b, precision=None):
    return lax.dot_general(
        a, b, (((1,), (1,)), ((), ())), precision=precision, preferred_element_type=F32
    )


def tn(a, b, precision=None):
    return lax.dot_general(
        a, b, (((0,), (0,)), ((), ())), precision=precision, preferred_element_type=F32
    )


def two_parts(x):
    high = x.astype(BF16)
    return high, (x - high.astype(F32)).astype(BF16)


def three_parts(x):
    high = x.astype(BF16)
    rest = x - high.astype(F32)
    middle = rest.astype(BF16)
    return high, middle, (rest - middle.astype(F32)).astype(BF16)


def covariance(points, anchors):
    products = tn(points, anchors, HIGHEST)
    norm_points = tn(points * points, jnp.ones((FEAT, TILE), F32), HIGHEST)[:, :1]
    norm_anchors = jnp.sum(anchors * anchors, axis=0, keepdims=True)
    distance = norm_points + norm_anchors - 2.0 * products
    return products * (1.0 / FEAT) + jnp.exp(distance * (-0.5 / FEAT))


def invert_factor(t_ref):
    ri = lax.broadcasted_iota(jnp.int32, (STRIP, TILE), 0)
    ci = lax.broadcasted_iota(jnp.int32, (STRIP, TILE), 1)
    rj = lax.broadcasted_iota(jnp.int32, (TILE, TILE), 0)
    cj = lax.broadcasted_iota(jnp.int32, (TILE, TILE), 1)

    def strip(k, carry):
        first = pl.multiple_of(k * STRIP, STRIP)
        rows = t_ref[pl.ds(first, STRIP), :]
        turned = pltpu.roll(rows, TILE - first, 1)
        cols = [jnp.broadcast_to(turned[:, c : c + 1], (STRIP, TILE)) for c in range(STRIP)]
        rows = jnp.where((ci >= first) & (ci < first + STRIP), (ci - first == ri).astype(F32), rows)
        pivots = jnp.ones((STRIP, TILE), F32)
        for c in range(STRIP):
            pivot = jnp.broadcast_to(cols[c][c : c + 1, :], (STRIP, TILE))
            pivots = jnp.where(ri == c, pivot, pivots)
            factor = jnp.where(ri > c, cols[c] * (1.0 / pivot), 0.0)
            for d in range(c + 1, STRIP):
                cols[d] = cols[d] - factor * cols[d][c : c + 1, :]
            rows = rows - factor * rows[c : c + 1, :]
        scale = lax.rsqrt(pivots)
        scale = scale * (1.5 - 0.5 * pivots * scale * scale)
        rows = rows * scale
        lh, lm, ll = three_parts(jnp.where(ci >= first + STRIP, rows, 0.0))
        rh, rm, rl = three_parts(rows)
        change = tn(
            jnp.concatenate([lh, lh, lm, lh, lm, ll], 0),
            jnp.concatenate([rh, rm, rh, rl, rm, rh], 0),
        )
        below = (cj >= first) & (cj < first + STRIP) & (rj >= first + STRIP)
        t_ref[...] = jnp.where(below, 0.0, t_ref[...]) - change
        t_ref[pl.ds(first, STRIP), :] = jnp.where(ci < first + STRIP, rows, 0.0)
        return carry

    lax.fori_loop(0, TILE // STRIP, strip, 0)


def body(
    feat_ref, factor_ref, out_ref,
    stage, high, low, land, feat_land, sums, parts, gram, gram_parts, gram_all, lower, tile, slab_kernel,
    stage_sem, piece_send, piece_recv, feat_send, feat_recv, low_send, low_recv,
    part_send, part_recv, gram_send, gram_recv,
):
    row, col = lax.axis_index("row"), lax.axis_index("col")
    x, z = row // 4, row % 4
    near = [((x + 1) % 4) * 4 + z, x * 4 + (z + 1) % 4, ((x + 3) % 4) * 4 + z, x * 4 + (z + 3) % 4]
    codes = [pick(row, table) for table in TREES]
    depth = [code // 16 for code in codes]
    sends = [[(code // (1 << d)) % 2 for d in range(4)] for code in codes]
    peers = [(col + n) % 8 for n in range(1, 8)]

    barrier = pltpu.get_barrier_semaphore()
    for d in range(4):
        pl.semaphore_signal(barrier, inc=1, device_id=(near[d], col), device_id_type=MESH)
    for peer in peers:
        pl.semaphore_signal(barrier, inc=1, device_id=(row, peer), device_id_type=MESH)
    pl.semaphore_wait(barrier, 11)

    def remote(src, dst, send, recv, device):
        return pltpu.make_async_remote_copy(
            src_ref=src, dst_ref=dst, send_sem=send, recv_sem=recv, device_id=device, device_id_type=MESH
        )

    def arrived(ref, sem):
        pltpu.make_async_copy(ref, ref, sem).wait()

    def piece_at(n, t):
        return land.at[n, pl.ds(t * SUB, SUB), :]

    def low_at(j, t):
        size = SUB * (4 - j)
        return lower.at[pl.ds(COLUMN[j] + t * size, size), :]

    def send_piece(src, n, t, d):
        remote(src, piece_at(n, t), piece_send.at[t, d], piece_recv.at[n, t], (near[d], col)).start()

    def send_features(src, t, d):
        remote(src, feat_land.at[t], feat_send.at[t, d], feat_recv.at[t], (near[d], col)).start()

    def send_low(j, t, d):
        remote(low_at(j, t), low_at(j, t), low_send.at[t, d], low_recv.at[j, t], (near[d], col)).start()

    def accumulate(slab, block, first, panel):
        panel_high, panel_low = panel
        both = jnp.concatenate([panel_high, panel_low], 0)
        a = nt(high[slab, pl.ds(first, 256), :], both)
        b = nt(low[slab, pl.ds(first, 256), :], panel_high)
        sums[block, pl.ds(first, 256), :] += a[:, :TILE] + a[:, TILE:] + b

    def send_parts(block):
        for peer in peers:
            src = sums.at[block, pl.ds(pl.multiple_of(peer * TILE, TILE), TILE), :]
            remote(src, parts.at[col, block], part_send, part_recv.at[col, block], (row, peer)).start()

    def own_points():
        return feat_ref[:, pl.ds(pl.multiple_of(col * TILE, TILE), TILE)]

    sums[...] = jnp.zeros_like(sums)

    @pl.when(row == 0)
    def root():
        for t in range(4):
            send_features(feat_ref.at[pl.ds(32 * t, 40), pl.ds(0, B)], t, t)

        def start_pieces(n, carry):
            block, slab = n // SLABS, n % SLABS
            for t in range(4):
                src = factor_ref.at[
                    pl.ds(pl.multiple_of(block * TILE + t * SUB, SUB), SUB),
                    pl.ds(pl.multiple_of(slab * SLAB, SLAB), SLAB),
                ]
                send_piece(src, n, t, t)
            return carry

        lax.fori_loop(0, PIECES, start_pieces, 0)

        def load(half, slab):
            return pltpu.make_async_copy(
                factor_ref.at[pl.ds(half * 512, 512), pl.ds(pl.multiple_of(slab * SLAB, SLAB), SLAB)],
                stage.at[slab % 2, pl.ds(half * 512, 512), :],
                stage_sem.at[half, slab % 2],
            )

        def product(half):
            load(half, 0).start()
            load(half, 1).start()

            def one(slab, carry):
                load(half, slab).wait()
                h, l = two_parts(stage[slab % 2, pl.ds(half * 512, 512), :])
                high[slab, pl.ds(half * 512, 512), :] = h
                low[slab, pl.ds(half * 512, 512), :] = l

                @pl.when(slab + 2 < SLABS)
                def _():
                    load(half, slab + 2).start()

                def block_rows(q, carry):
                    block, tile_rows = q // 2, q % 2
                    at = pl.ds(pl.multiple_of(block * TILE, TILE), TILE)
                    first = pl.multiple_of(half * 512 + tile_rows * 256, 256)
                    accumulate(slab, block, first, (high[slab, at, :], low[slab, at, :]))
                    return carry

                return lax.fori_loop(0, 8, block_rows, carry)

            lax.fori_loop(0, SLABS, one, 0)

        product(0)
        for n, (i, j) in enumerate(BLOCKS):
            gram[pl.ds(n * TILE, TILE), :] = sums[j, pl.ds(i * TILE, TILE), :]
        mine = pl.ds(pl.multiple_of(col * SHARE, SHARE), SHARE)
        for peer in peers:
            src = gram.at[pl.ds(pl.multiple_of(peer * SHARE, SHARE), SHARE), :]
            remote(src, gram_parts.at[col], gram_send.at[0], gram_recv.at[0, col], (row, peer)).start()
        product(1)
        share = gram[mine, :]
        for peer in peers:
            arrived(gram_parts.at[peer], gram_recv.at[0, peer])
            share = share + gram_parts[peer]
        gram_all[mine, :] = share
        for peer in peers:
            remote(
                gram_all.at[mine, :], gram_all.at[mine, :], gram_send.at[1], gram_recv.at[1, col], (row, peer)
            ).start()
        for j in range(4):
            size = (4 - j) * TILE
            values = covariance(feat_ref[:, j * TILE : B], feat_ref[:, j * TILE : (j + 1) * TILE])
            same = lax.broadcasted_iota(jnp.int32, (size, TILE), 0) == lax.broadcasted_iota(jnp.int32, (size, TILE), 1)
            lower[pl.ds(COLUMN[j], size), :] = values + jnp.where(same, RIDGE, 0.0)
        slab_kernel[...] = covariance(own_points(), feat_ref[:, :B])
        for peer in peers:
            arrived(gram_all.at[pl.ds(pl.multiple_of(peer * SHARE, SHARE), SHARE), :], gram_recv.at[1, peer])
        lower[...] = lower[...] - gram_all[...]
        for block in range(4):
            send_parts(block)

        def at(i, j):
            return pl.ds(PLACE[i, j] * TILE, TILE)

        for j in range(4):
            tile[...] = lower[at(j, j), :]
            invert_factor(tile)
            inverse = tile[...]
            lower[at(j, j), :] = inverse
            for i in range(j + 1, 4):
                lower[at(i, j), :] = nt(lower[at(i, j), :], inverse, HIGHEST)
            for t in range(4):
                send_low(j, t, t)
            for k in range(j + 1, 4):
                for i in range(k, 4):
                    lower[at(i, k), :] = lower[at(i, k), :] - nt(lower[at(i, j), :], lower[at(k, j), :], HIGHEST)

    @pl.when(row != 0)
    def others():
        def load(slab):
            return pltpu.make_async_copy(
                factor_ref.at[:, pl.ds(pl.multiple_of(slab * SLAB, SLAB), SLAB)],
                stage.at[slab % 2],
                stage_sem.at[0, slab % 2],
            )

        load(0).start()
        load(1).start()

        def slot(s, carry):
            for t in range(4):
                item = s - SKEW * depth[t]

                @pl.when(item == 0)
                def _():
                    arrived(feat_land.at[t], feat_recv.at[t])
                    for d in range(4):
                        @pl.when(sends[t][d] == 1)
                        def _():
                            send_features(feat_land.at[t], t, d)

                @pl.when((item >= 1) & (item <= PIECES))
                def _():
                    n = item - 1
                    arrived(piece_at(n, t), piece_recv.at[n, t])
                    for d in range(4):
                        @pl.when(sends[t][d] == 1)
                        def _():
                            send_piece(piece_at(n, t), n, t, d)

                for j in range(4):
                    @pl.when(item == PIECES + 1 + j)
                    def _():
                        arrived(low_at(j, t), low_recv.at[j, t])
                        for d in range(4):
                            @pl.when(sends[t][d] == 1)
                            def _():
                                send_low(j, t, d)

            @pl.when(s < SLABS)
            def _():
                load(s).wait()
                h, l = two_parts(stage[s % 2])
                high[s] = h
                low[s] = l

                @pl.when(s + 2 < SLABS)
                def _():
                    load(s + 2).start()

            @pl.when(s == SKEW * DEPTH)
            def _():
                anchors = jnp.concatenate([feat_land[t, :32] for t in range(3)] + [feat_land[3]], 0)
                slab_kernel[...] = covariance(own_points(), anchors)

            m = s - SKEW * DEPTH - 1

            @pl.when((m >= 0) & (m < PIECES))
            def _():
                block, slab = m // SLABS, m % SLABS
                panel = two_parts(land[m])

                def tile_rows(q, carry):
                    accumulate(slab, block, pl.multiple_of(q * 256, 256), panel)
                    return carry

                lax.fori_loop(0, ROWS // 256, tile_rows, 0)

                @pl.when(slab == SLABS - 1)
                def _():
                    send_parts(block)

            return carry

        lax.fori_loop(0, SLOTS, slot, 0)

    solved = []
    rows = lax.broadcasted_iota(jnp.int32, (TILE, TILE), 0) + row * ROWS + col * TILE
    columns = lax.broadcasted_iota(jnp.int32, (TILE, TILE), 1)
    for j in range(4):
        value = slab_kernel[:, j * TILE : (j + 1) * TILE]
        value = value + jnp.where(rows == columns + j * TILE, RIDGE, 0.0)
        total = sums[j, pl.ds(pl.multiple_of(col * TILE, TILE), TILE), :]
        for peer in peers:
            arrived(parts.at[peer, j], part_recv.at[peer, j])
            total = total + parts[peer, j]
        value = value - total
        for i in range(j):
            value = value - nt(solved[i], lower[pl.ds(PLACE[j, i] * TILE, TILE), :], HIGHEST)
        solved.append(nt(value, lower[pl.ds(PLACE[j, j] * TILE, TILE), :], HIGHEST))
        out_ref[:, j * TILE : (j + 1) * TILE] = solved[j]

    arrived(sums.at[:, pl.ds(0, 7 * TILE), :], part_send)
    for t in range(4):
        for d in range(4):
            @pl.when(sends[t][d] == 1)
            def _():
                arrived(land.at[:, pl.ds(0, SUB), :], piece_send.at[t, d])
                arrived(feat_land.at[t], feat_send.at[t, d])
                arrived(lower.at[pl.ds(0, 10 * SUB), :], low_send.at[t, d])

    @pl.when(row == 0)
    def _():
        for phase in range(2):
            arrived(gram_parts.at[pl.ds(0, 7)], gram_send.at[phase])


def on_device(features, factor):
    dma = pltpu.SemaphoreType.DMA
    return pl.pallas_call(
        body,
        out_shape=jax.ShapeDtypeStruct((TILE, B), F32),
        in_specs=[pl.BlockSpec(memory_space=pltpu.VMEM), pl.BlockSpec(memory_space=pl.ANY)],
        out_specs=pl.BlockSpec(memory_space=pltpu.VMEM),
        scratch_shapes=[
            pltpu.VMEM((2, ROWS, SLAB), F32),
            pltpu.VMEM((SLABS, ROWS, SLAB), BF16),
            pltpu.VMEM((SLABS, ROWS, SLAB), BF16),
            pltpu.VMEM((PIECES, TILE, SLAB), F32),
            pltpu.VMEM((4, 40, B), F32),
            pltpu.VMEM((4, ROWS, TILE), F32),
            pltpu.VMEM((8, 4, TILE, TILE), F32),
            pltpu.VMEM((10 * TILE, TILE), F32),
            pltpu.VMEM((8, SHARE, TILE), F32),
            pltpu.VMEM((10 * TILE, TILE), F32),
            pltpu.VMEM((10 * TILE, TILE), F32),
            pltpu.VMEM((TILE, TILE), F32),
            pltpu.VMEM((TILE, B), F32),
            dma((2, 2)),
            dma((4, 4)),
            dma((PIECES, 4)),
            dma((4, 4)),
            dma((4,)),
            dma((4, 4)),
            dma((4, 4)),
            dma,
            dma((8, 4)),
            dma((2,)),
            dma((2, 8)),
        ],
        compiler_params=pltpu.CompilerParams(
            collective_id=0, has_side_effects=True, vmem_limit_bytes=56 << 20
        ),
    )(features, factor)


def solution(mesh):
    placed = (P(None, "row"), P("row", "col"))
    return jax.shard_map(
        on_device, mesh=mesh, in_specs=placed, out_specs=P(("row", "col"), None), check_vma=False
    )
```

profile of v0, /device:TPU:3, one launch (start us, length us, event | category | flops | bytes accessed | tf_op | source)
XLA Modules:
  0.0 118.7 jit_solution(17378111619871976251)
XLA Ops:
  0.0 117.0 %shard_map.28 = f32[128,512]{1,0:T(8,128)} custom-call(f32[136,1024]{1,0:T(8,128)} %feat_ref.1, f32[1024,4096]{1,0:T(8,128)} %factor_ref.1), custom_call_target="tpu_custom_call" | custom-call | tf_op jit(solution)/shard_map/pallas_call | solution.py:385
  117.0 1.7 %copy.4 = f32[128,512]{1,0:T(8,128)} copy(f32[128,512]{1,0:T(8,128)} %shard_map.28) | data formatting | bytes 524288
where the time goes:
time: 119 us
  Pallas kernels  117 us (98%)
  local copies, waits for them, and re-layouts  1.67 us (1%)
    pallas_call x1, Pallas kernels, on_device(): pl.pallas_call(body, out_shape=jax.ShapeDtypeStruct((TILE, B), F32), in_s...  117 us

commit v1 on v0

--- a/solution.py
+++ b/solution.py
@@ -21,6 +21,7 @@
 SLABS = 8
 PIECES = 32
 SUB = 32
+AHEAD = 8
 SKEW = 3
 DEPTH = 5
 ITEMS = 1 + PIECES + 4
@@ -116,9 +117,9 @@
 
 def body(
     feat_ref, factor_ref, out_ref,
-    stage, high, low, land, feat_land, sums, parts, gram, gram_parts, gram_all, lower, tile, slab_kernel,
+    stage, high, low, land, feat_land, sums, pair, parts, own, gram, gram_parts, gram_all, lower, tile, slab_kernel,
     stage_sem, piece_send, piece_recv, feat_send, feat_recv, low_send, low_recv,
-    part_send, part_recv, gram_send, gram_recv,
+    pair_send, pair_recv, part_send, part_recv, gram_send, gram_recv,
 ):
     row, col = lax.axis_index("row"), lax.axis_index("col")
     x, z = row // 4, row % 4
@@ -127,6 +128,9 @@
     depth = [code // 16 for code in codes]
     sends = [[(code // (1 << d)) % 2 for d in range(4)] for code in codes]
     peers = [(col + n) % 8 for n in range(1, 8)]
+    y, core = col // 2, col % 2
+    sibling = y * 2 + 1 - core
+    pivot = (row == 0) & (col < 4)
 
     barrier = pltpu.get_barrier_semaphore()
     for d in range(4):
@@ -159,17 +163,29 @@
     def send_low(j, t, d):
         remote(low_at(j, t), low_at(j, t), low_send.at[t, d], low_recv.at[j, t], (near[d], col)).start()
 
-    def accumulate(slab, block, first, panel):
+    def accumulate(slab, block, panel):
         panel_high, panel_low = panel
-        both = jnp.concatenate([panel_high, panel_low], 0)
-        a = nt(high[slab, pl.ds(first, 256), :], both)
-        b = nt(low[slab, pl.ds(first, 256), :], panel_high)
-        sums[block, pl.ds(first, 256), :] += a[:, :TILE] + a[:, TILE:] + b
-
-    def send_parts(block):
-        for peer in peers:
-            src = sums.at[block, pl.ds(pl.multiple_of(peer * TILE, TILE), TILE), :]
-            remote(src, parts.at[col, block], part_send, part_recv.at[col, block], (row, peer)).start()
+        a = nt(high[slab], jnp.concatenate([panel_high, panel_low], 0))
+        b = nt(low[slab], panel_high)
+        sums[block] += a[:, :TILE] + a[:, TILE:] + b
+
+    def owned(q, c):
+        return pl.ds(pl.multiple_of((q * 2 + c) * TILE, TILE), TILE)
+
+    def send_pair(block, first):
+        for q in range(first, 4):
+            src = sums.at[block, owned(q, 1 - core), :]
+            remote(src, pair.at[block, q], pair_send, pair_recv.at[block], (row, sibling)).start()
+
+    def send_parts(block, first):
+        arrived(pair.at[block, pl.ds(first, 4 - first)], pair_recv.at[block])
+        for q in range(first, 4):
+            sums[block, owned(q, core), :] += pair[block, q]
+
+            @pl.when(q != y)
+            def _():
+                src = sums.at[block, owned(q, core), :]
+                remote(src, parts.at[block, y], part_send, part_recv.at[block, y], (row, q * 2 + core)).start()
 
     def own_points():
         return feat_ref[:, pl.ds(pl.multiple_of(col * TILE, TILE), TILE)]
@@ -181,7 +197,7 @@
         for t in range(4):
             send_features(feat_ref.at[pl.ds(32 * t, 40), pl.ds(0, B)], t, t)
 
-        def start_pieces(n, carry):
+        def start_piece(n, carry):
             block, slab = n // SLABS, n % SLABS
             for t in range(4):
                 src = factor_ref.at[
@@ -191,7 +207,7 @@
                 send_piece(src, n, t, t)
             return carry
 
-        lax.fori_loop(0, PIECES, start_pieces, 0)
+        lax.fori_loop(0, AHEAD, start_piece, 0)
 
         def load(half, slab):
             return pltpu.make_async_copy(
@@ -200,11 +216,10 @@
                 stage_sem.at[half, slab % 2],
             )
 
-        def product(half):
-            load(half, 0).start()
-            load(half, 1).start()
-
+        def product(half, begin, end):
             def one(slab, carry):
+                if half == 0:
+                    carry = lax.fori_loop(AHEAD + slab * 3, AHEAD + slab * 3 + 3, start_piece, carry)
                 load(half, slab).wait()
                 h, l = two_parts(stage[slab % 2, pl.ds(half * 512, 512), :])
                 high[slab, pl.ds(half * 512, 512), :] = h
@@ -214,25 +229,28 @@
                 def _():
                     load(half, slab + 2).start()
 
-                def block_rows(q, carry):
-                    block, tile_rows = q // 2, q % 2
-                    at = pl.ds(pl.multiple_of(block * TILE, TILE), TILE)
-                    first = pl.multiple_of(half * 512 + tile_rows * 256, 256)
-                    accumulate(slab, block, first, (high[slab, at, :], low[slab, at, :]))
-                    return carry
-
-                return lax.fori_loop(0, 8, block_rows, carry)
-
-            lax.fori_loop(0, SLABS, one, 0)
-
-        product(0)
+                panel_high, panel_low = high[slab, :512], low[slab, :512]
+                if half == 0:
+                    total = nt(h, panel_high * 0.5) + nt(h, panel_low)
+                else:
+                    total = nt(h, panel_high) + nt(h, panel_low) + nt(l, panel_high)
+                for block in range(4):
+                    sums[block, pl.ds(half * 512, 512), :] += total[:, block * TILE : (block + 1) * TILE]
+                return carry
+
+            lax.fori_loop(begin, end, one, 0)
+
+        for half in range(2):
+            load(half, 0).start()
+            load(half, 1).start()
+        product(0, 0, SLABS)
         for n, (i, j) in enumerate(BLOCKS):
-            gram[pl.ds(n * TILE, TILE), :] = sums[j, pl.ds(i * TILE, TILE), :]
+            gram[pl.ds(n * TILE, TILE), :] = sums[j, pl.ds(i * TILE, TILE), :] + sums[i, pl.ds(j * TILE, TILE), :].T
         mine = pl.ds(pl.multiple_of(col * SHARE, SHARE), SHARE)
         for peer in peers:
             src = gram.at[pl.ds(pl.multiple_of(peer * SHARE, SHARE), SHARE), :]
             remote(src, gram_parts.at[col], gram_send.at[0], gram_recv.at[0, col], (row, peer)).start()
-        product(1)
+        product(1, 0, 4)
         share = gram[mine, :]
         for peer in peers:
             arrived(gram_parts.at[peer], gram_recv.at[0, peer])
@@ -247,12 +265,9 @@
             values = covariance(feat_ref[:, j * TILE : B], feat_ref[:, j * TILE : (j + 1) * TILE])
             same = lax.broadcasted_iota(jnp.int32, (size, TILE), 0) == lax.broadcasted_iota(jnp.int32, (size, TILE), 1)
             lower[pl.ds(COLUMN[j], size), :] = values + jnp.where(same, RIDGE, 0.0)
-        slab_kernel[...] = covariance(own_points(), feat_ref[:, :B])
         for peer in peers:
             arrived(gram_all.at[pl.ds(pl.multiple_of(peer * SHARE, SHARE), SHARE), :], gram_recv.at[1, peer])
         lower[...] = lower[...] - gram_all[...]
-        for block in range(4):
-            send_parts(block)
 
         def at(i, j):
             return pl.ds(PLACE[i, j] * TILE, TILE)
@@ -269,6 +284,12 @@
             for k in range(j + 1, 4):
                 for i in range(k, 4):
                     lower[at(i, k), :] = lower[at(i, k), :] - nt(lower[at(i, j), :], lower[at(k, j), :], HIGHEST)
+        product(1, 4, SLABS)
+        for block in range(4):
+            send_pair(block, 2)
+        slab_kernel[...] = covariance(own_points(), feat_ref[:, :B])
+        for block in range(4):
+            send_parts(block, 2)
 
     @pl.when(row != 0)
     def others():
@@ -333,17 +354,15 @@
             @pl.when((m >= 0) & (m < PIECES))
             def _():
                 block, slab = m // SLABS, m % SLABS
-                panel = two_parts(land[m])
-
-                def tile_rows(q, carry):
-                    accumulate(slab, block, pl.multiple_of(q * 256, 256), panel)
-                    return carry
-
-                lax.fori_loop(0, ROWS // 256, tile_rows, 0)
+                accumulate(slab, block, two_parts(land[m]))
 
                 @pl.when(slab == SLABS - 1)
                 def _():
-                    send_parts(block)
+                    send_pair(block, 0)
+
+                @pl.when((slab == 1) & (block > 0))
+                def _():
+                    send_parts(block - 1, 0)
 
             return carry
 
@@ -352,20 +371,59 @@
     solved = []
     rows = lax.broadcasted_iota(jnp.int32, (TILE, TILE), 0) + row * ROWS + col * TILE
     columns = lax.broadcasted_iota(jnp.int32, (TILE, TILE), 1)
-    for j in range(4):
+
+    def rest(j):
         value = slab_kernel[:, j * TILE : (j + 1) * TILE]
         value = value + jnp.where(rows == columns + j * TILE, RIDGE, 0.0)
-        total = sums[j, pl.ds(pl.multiple_of(col * TILE, TILE), TILE), :]
-        for peer in peers:
-            arrived(parts.at[peer, j], part_recv.at[peer, j])
-            total = total + parts[peer, j]
-        value = value - total
         for i in range(j):
             value = value - nt(solved[i], lower[pl.ds(PLACE[j, i] * TILE, TILE), :], HIGHEST)
-        solved.append(nt(value, lower[pl.ds(PLACE[j, j] * TILE, TILE), :], HIGHEST))
-        out_ref[:, j * TILE : (j + 1) * TILE] = solved[j]
-
-    arrived(sums.at[:, pl.ds(0, 7 * TILE), :], part_send)
+        return value
+
+    def solve(j, value):
+        @pl.when(pivot)
+        def _():
+            place = COLUMN[j] + jnp.maximum(col - j, 0) * TILE
+            own[...] = gram_all[pl.ds(pl.multiple_of(place, TILE), TILE), :]
+
+        @pl.when(jnp.logical_not(pivot))
+        def _():
+            own[...] = sums[j, owned(y, core), :]
+            for n in range(1, 4):
+                other = (y + n) % 4
+                arrived(parts.at[j, other], part_recv.at[j, other])
+                own[...] += parts[j, other]
+
+        value = nt(value - own[...], lower[pl.ds(PLACE[j, j] * TILE, TILE), :], HIGHEST)
+        value = jnp.where(pivot & (col < j), 0.0, value)
+        solved.append(value)
+        out_ref[:, j * TILE : (j + 1) * TILE] = value
+
+    solve(0, rest(0))
+
+    @pl.when(row != 0)
+    def _():
+        send_parts(3, 0)
+
+    for j in range(1, 4):
+        solve(j, rest(j))
+
+    @pl.when(row != 0)
+    def _():
+        arrived(pair, pair_send)
+        arrived(parts.at[:, pl.ds(0, 3)], part_send)
+
+    @pl.when(row == 0)
+    def _():
+        arrived(pair.at[:, pl.ds(0, 2)], pair_send)
+
+        @pl.when(pivot)
+        def _():
+            arrived(parts.at[:, pl.ds(0, 2)], part_send)
+
+        @pl.when(jnp.logical_not(pivot))
+        def _():
+            arrived(parts.at[:, 0], part_send)
+
     for t in range(4):
         for d in range(4):
             @pl.when(sends[t][d] == 1)
@@ -394,7 +452,9 @@
             pltpu.VMEM((PIECES, TILE, SLAB), F32),
             pltpu.VMEM((4, 40, B), F32),
             pltpu.VMEM((4, ROWS, TILE), F32),
-            pltpu.VMEM((8, 4, TILE, TILE), F32),
+            pltpu.VMEM((4, 4, TILE, TILE), F32),
+            pltpu.VMEM((4, 4, TILE, TILE), F32),
+            pltpu.VMEM((TILE, TILE), F32),
             pltpu.VMEM((10 * TILE, TILE), F32),
             pltpu.VMEM((8, SHARE, TILE), F32),
             pltpu.VMEM((10 * TILE, TILE), F32),
@@ -409,7 +469,9 @@
             dma((4, 4)),
             dma((4, 4)),
             dma,
-            dma((8, 4)),
+            dma((4,)),
+            dma,
+            dma((4, 4)),
             dma((2,)),
             dma((2, 8)),
         ],

time: 119 us -> 92.7 us (0.78)
  the two profiles are of different devices: /device:TPU:3 before, /device:TPU:2 now
where the time goes in v1:
time: 92.7 us; the launch traced here: 92.4 us
  Pallas kernels  90.7 us (98%)
  local copies, waits for them, and re-layouts  1.67 us (2%)
    pallas_call x1, Pallas kernels, on_device(): pl.pallas_call(body, out_shape=jax.ShapeDtypeStruct((TILE, B), F32), in_s...  90.7 us

profile of v1, /device:TPU:2, one launch (start us, length us, event | category | flops | bytes accessed | tf_op | source)
XLA Modules:
  0.0 92.4 jit_solution(5069997831046089278)
XLA Ops:
  0.0 90.7 %shard_map.28 = f32[128,512]{1,0:T(8,128)} custom-call(f32[136,1024]{1,0:T(8,128)} %feat_ref.1, f32[1024,4096]{1,0:T(8,128)} %factor_ref.1), custom_call_target="tpu_custom_call" | custom-call | tf_op jit(solution)/shard_map/pallas_call | solution.py:443
  90.7 1.7 %copy.4 = f32[128,512]{1,0:T(8,128)} copy(f32[128,512]{1,0:T(8,128)} %shard_map.28) | data formatting | bytes 524288

commit v2 on v1

--- a/solution.py
+++ b/solution.py
@@ -22,10 +22,7 @@
 PIECES = 32
 SUB = 32
 AHEAD = 8
-SKEW = 3
-DEPTH = 5
-ITEMS = 1 + PIECES + 4
-SLOTS = ITEMS + SKEW * DEPTH
+ITEMS = PIECES + 1 + 4
 
 TREES = (
     (1, 48, 64, 48, 27, 39, 53, 36, 41, 49, 65, 49, 48, 64, 80, 64),
@@ -37,6 +34,10 @@
 PLACE = {b: n for n, b in enumerate(BLOCKS)}
 COLUMN = [PLACE[j, j] * TILE for j in range(4)]
 SHARE = len(BLOCKS) * TILE // 8
+
+
+def lag(depth):
+    return depth * 3 - 1
 
 
 def pick(index, table):
@@ -119,7 +120,7 @@
     feat_ref, factor_ref, out_ref,
     stage, high, low, land, feat_land, sums, pair, parts, own, gram, gram_parts, gram_all, lower, tile, slab_kernel,
     stage_sem, piece_send, piece_recv, feat_send, feat_recv, low_send, low_recv,
-    pair_send, pair_recv, part_send, part_recv, gram_send, gram_recv,
+    pair_send, pair_recv, part_send, part_recv, gram_send, gram_recv, share_send, share_recv,
 ):
     row, col = lax.axis_index("row"), lax.axis_index("col")
     x, z = row // 4, row % 4
@@ -131,6 +132,8 @@
     y, core = col // 2, col % 2
     sibling = y * 2 + 1 - core
     pivot = (row == 0) & (col < 4)
+    lags = [lag(d) for d in depth]
+    last = jnp.maximum(jnp.maximum(lags[0], lags[1]), jnp.maximum(lags[2], lags[3]))
 
     barrier = pltpu.get_barrier_semaphore()
     for d in range(4):
@@ -150,18 +153,24 @@
     def piece_at(n, t):
         return land.at[n, pl.ds(t * SUB, SUB), :]
 
-    def low_at(j, t):
-        size = SUB * (4 - j)
-        return lower.at[pl.ds(COLUMN[j] + t * size, size), :]
+    def low_at(j, t, c):
+        size = SUB // 2 * (4 - j)
+        return lower.at[pl.ds(pl.multiple_of(COLUMN[j] + (2 * t + c) * size, 16), size), :]
+
+    def feat_at(t, c):
+        return feat_land.at[t, :, pl.ds(pl.multiple_of(c * (B // 2), TILE), B // 2)]
+
+    def exchange(ref, item, t):
+        remote(ref, ref, share_send, share_recv.at[item, t], (row, sibling)).start()
 
     def send_piece(src, n, t, d):
         remote(src, piece_at(n, t), piece_send.at[t, d], piece_recv.at[n, t], (near[d], col)).start()
 
     def send_features(src, t, d):
-        remote(src, feat_land.at[t], feat_send.at[t, d], feat_recv.at[t], (near[d], col)).start()
+        remote(src, feat_at(t, core), feat_send.at[t, d], feat_recv.at[t], (near[d], col)).start()
 
     def send_low(j, t, d):
-        remote(low_at(j, t), low_at(j, t), low_send.at[t, d], low_recv.at[j, t], (near[d], col)).start()
+        remote(low_at(j, t, core), low_at(j, t, core), low_send.at[t, d], low_recv.at[j, t], (near[d], col)).start()
 
     def accumulate(slab, block, panel):
         panel_high, panel_low = panel
@@ -190,13 +199,8 @@
     def own_points():
         return feat_ref[:, pl.ds(pl.multiple_of(col * TILE, TILE), TILE)]
 
-    sums[...] = jnp.zeros_like(sums)
-
     @pl.when(row == 0)
     def root():
-        for t in range(4):
-            send_features(feat_ref.at[pl.ds(32 * t, 40), pl.ds(0, B)], t, t)
-
         def start_piece(n, carry):
             block, slab = n // SLABS, n % SLABS
             for t in range(4):
@@ -208,6 +212,7 @@
             return carry
 
         lax.fori_loop(0, AHEAD, start_piece, 0)
+        sums[...] = jnp.zeros_like(sums)
 
         def load(half, slab):
             return pltpu.make_async_copy(
@@ -244,6 +249,9 @@
             load(half, 0).start()
             load(half, 1).start()
         product(0, 0, SLABS)
+        for t in range(4):
+            half = pl.ds(pl.multiple_of(core * (B // 2), TILE), B // 2)
+            send_features(feat_ref.at[pl.ds(32 * t, 40), half], t, t)
         for n, (i, j) in enumerate(BLOCKS):
             gram[pl.ds(n * TILE, TILE), :] = sums[j, pl.ds(i * TILE, TILE), :] + sums[i, pl.ds(j * TILE, TILE), :].T
         mine = pl.ds(pl.multiple_of(col * SHARE, SHARE), SHARE)
@@ -302,36 +310,40 @@
 
         load(0).start()
         load(1).start()
+        sums[...] = jnp.zeros_like(sums)
 
         def slot(s, carry):
             for t in range(4):
-                item = s - SKEW * depth[t]
-
-                @pl.when(item == 0)
+                item = s - lags[t]
+
+                @pl.when((item >= 0) & (item < PIECES))
                 def _():
-                    arrived(feat_land.at[t], feat_recv.at[t])
+                    arrived(piece_at(item, t), piece_recv.at[item, t])
                     for d in range(4):
                         @pl.when(sends[t][d] == 1)
                         def _():
-                            send_features(feat_land.at[t], t, d)
-
-                @pl.when((item >= 1) & (item <= PIECES))
+                            send_piece(piece_at(item, t), item, t, d)
+
+                @pl.when((item >= PIECES) & (item < ITEMS))
                 def _():
-                    n = item - 1
-                    arrived(piece_at(n, t), piece_recv.at[n, t])
-                    for d in range(4):
-                        @pl.when(sends[t][d] == 1)
-                        def _():
-                            send_piece(piece_at(n, t), n, t, d)
-
-                for j in range(4):
-                    @pl.when(item == PIECES + 1 + j)
+                    @pl.when(item == PIECES)
                     def _():
-                        arrived(low_at(j, t), low_recv.at[j, t])
+                        arrived(feat_at(t, core), feat_recv.at[t])
                         for d in range(4):
                             @pl.when(sends[t][d] == 1)
                             def _():
-                                send_low(j, t, d)
+                                send_features(feat_at(t, core), t, d)
+                        exchange(feat_at(t, core), 4, t)
+
+                    for j in range(4):
+                        @pl.when(item == PIECES + 1 + j)
+                        def _():
+                            arrived(low_at(j, t, core), low_recv.at[j, t])
+                            for d in range(4):
+                                @pl.when(sends[t][d] == 1)
+                                def _():
+                                    send_low(j, t, d)
+                            exchange(low_at(j, t, core), j, t)
 
             @pl.when(s < SLABS)
             def _():
@@ -344,12 +356,18 @@
                 def _():
                     load(s + 2).start()
 
-            @pl.when(s == SKEW * DEPTH)
+            m = s - last
+
+            @pl.when(m == PIECES)
             def _():
+                send_parts(3, 0)
+
+            @pl.when(m == PIECES + 2)
+            def _():
+                for t in range(4):
+                    arrived(feat_at(t, 1 - core), share_recv.at[4, t])
                 anchors = jnp.concatenate([feat_land[t, :32] for t in range(3)] + [feat_land[3]], 0)
                 slab_kernel[...] = covariance(own_points(), anchors)
-
-            m = s - SKEW * DEPTH - 1
 
             @pl.when((m >= 0) & (m < PIECES))
             def _():
@@ -366,13 +384,18 @@
 
             return carry
 
-        lax.fori_loop(0, SLOTS, slot, 0)
+        lax.fori_loop(0, ITEMS + last, slot, 0)
 
     solved = []
     rows = lax.broadcasted_iota(jnp.int32, (TILE, TILE), 0) + row * ROWS + col * TILE
     columns = lax.broadcasted_iota(jnp.int32, (TILE, TILE), 1)
 
     def rest(j):
+        @pl.when(row != 0)
+        def _():
+            for t in range(4):
+                arrived(low_at(j, t, 1 - core), share_recv.at[j, t])
+
         value = slab_kernel[:, j * TILE : (j + 1) * TILE]
         value = value + jnp.where(rows == columns + j * TILE, RIDGE, 0.0)
         for i in range(j):
@@ -398,17 +421,13 @@
         solved.append(value)
         out_ref[:, j * TILE : (j + 1) * TILE] = value
 
-    solve(0, rest(0))
+    for j in range(4):
+        solve(j, rest(j))
 
     @pl.when(row != 0)
     def _():
-        send_parts(3, 0)
-
-    for j in range(1, 4):
-        solve(j, rest(j))
-
-    @pl.when(row != 0)
-    def _():
+        arrived(feat_land.at[:, :, pl.ds(0, B // 2)], share_send)
+        arrived(lower.at[pl.ds(0, 5 * TILE), :], share_send)
         arrived(pair, pair_send)
         arrived(parts.at[:, pl.ds(0, 3)], part_send)
 
@@ -429,8 +448,8 @@
             @pl.when(sends[t][d] == 1)
             def _():
                 arrived(land.at[:, pl.ds(0, SUB), :], piece_send.at[t, d])
-                arrived(feat_land.at[t], feat_send.at[t, d])
-                arrived(lower.at[pl.ds(0, 10 * SUB), :], low_send.at[t, d])
+                arrived(feat_at(t, 0), feat_send.at[t, d])
+                arrived(lower.at[pl.ds(0, 5 * SUB), :], low_send.at[t, d])
 
     @pl.when(row == 0)
     def _():
@@ -474,6 +493,8 @@
             dma((4, 4)),
             dma((2,)),
             dma((2, 8)),
+            dma,
+            dma((5, 4)),
         ],
         compiler_params=pltpu.CompilerParams(
             collective_id=0, has_side_effects=True, vmem_limit_bytes=56 << 20

time: 92.7 us -> 82.2 us (0.89)
  the two profiles are of different devices: /device:TPU:2 before, /device:TPU:37 now
where the time goes in v2:
time: 82.2 us; the launch traced here: 81.9 us
  Pallas kernels  80.2 us (98%)
  local copies, waits for them, and re-layouts  1.67 us (2%)
    pallas_call x1, Pallas kernels, on_device(): pl.pallas_call(body, out_shape=jax.ShapeDtypeStruct((TILE, B), F32), in_s...  80.2 us
    unnamed x1, local copies, waits for them, and re-layouts  1.67 us

profile of v2, /device:TPU:37, one launch (start us, length us, event | category | flops | bytes accessed | tf_op | source)
XLA Modules:
  0.0 81.9 jit_solution(14778158198960698806)
XLA Ops:
  0.0 80.2 %shard_map.28 = f32[128,512]{1,0:T(8,128)} custom-call(f32[136,1024]{1,0:T(8,128)} %feat_ref.1, f32[1024,4096]{1,0:T(8,128)} %factor_ref.1), custom_call_target="tpu_custom_call" | custom-call | tf_op jit(solution)/shard_map/pallas_call | solution.py:462
  80.2 1.7 %copy.4 = f32[128,512]{1,0:T(8,128)} copy(f32[128,512]{1,0:T(8,128)} %shard_map.28) | data formatting | bytes 524288

commit v3 on v2

--- a/solution.py
+++ b/solution.py
@@ -119,7 +119,7 @@
 def body(
     feat_ref, factor_ref, out_ref,
     stage, high, low, land, feat_land, sums, pair, parts, own, gram, gram_parts, gram_all, lower, tile, slab_kernel,
-    stage_sem, piece_send, piece_recv, feat_send, feat_recv, low_send, low_recv,
+    points, pivots, points_sem, stage_sem, piece_send, piece_recv, feat_send, feat_recv, low_send, low_recv,
     pair_send, pair_recv, part_send, part_recv, gram_send, gram_recv, share_send, share_recv,
 ):
     row, col = lax.axis_index("row"), lax.axis_index("col")
@@ -196,8 +196,10 @@
                 src = sums.at[block, owned(q, core), :]
                 remote(src, parts.at[block, y], part_send, part_recv.at[block, y], (row, q * 2 + core)).start()
 
-    def own_points():
-        return feat_ref[:, pl.ds(pl.multiple_of(col * TILE, TILE), TILE)]
+    own_points = pltpu.make_async_copy(
+        feat_ref.at[:, pl.ds(pl.multiple_of(col * TILE, TILE), TILE)], points, points_sem.at[0]
+    )
+    own_points.start()
 
     @pl.when(row == 0)
     def root():
@@ -245,6 +247,8 @@
 
             lax.fori_loop(begin, end, one, 0)
 
+        pivot_points = pltpu.make_async_copy(feat_ref.at[:, pl.ds(0, B)], pivots, points_sem.at[1])
+        pivot_points.start()
         for half in range(2):
             load(half, 0).start()
             load(half, 1).start()
@@ -268,9 +272,10 @@
             remote(
                 gram_all.at[mine, :], gram_all.at[mine, :], gram_send.at[1], gram_recv.at[1, col], (row, peer)
             ).start()
+        pivot_points.wait()
         for j in range(4):
             size = (4 - j) * TILE
-            values = covariance(feat_ref[:, j * TILE : B], feat_ref[:, j * TILE : (j + 1) * TILE])
+            values = covariance(pivots[:, j * TILE : B], pivots[:, j * TILE : (j + 1) * TILE])
             same = lax.broadcasted_iota(jnp.int32, (size, TILE), 0) == lax.broadcasted_iota(jnp.int32, (size, TILE), 1)
             lower[pl.ds(COLUMN[j], size), :] = values + jnp.where(same, RIDGE, 0.0)
         for peer in peers:
@@ -295,7 +300,8 @@
         product(1, 4, SLABS)
         for block in range(4):
             send_pair(block, 2)
-        slab_kernel[...] = covariance(own_points(), feat_ref[:, :B])
+        own_points.wait()
+        slab_kernel[...] = covariance(points[...], pivots[...])
         for block in range(4):
             send_parts(block, 2)
 
@@ -367,7 +373,8 @@
                 for t in range(4):
                     arrived(feat_at(t, 1 - core), share_recv.at[4, t])
                 anchors = jnp.concatenate([feat_land[t, :32] for t in range(3)] + [feat_land[3]], 0)
-                slab_kernel[...] = covariance(own_points(), anchors)
+                own_points.wait()
+                slab_kernel[...] = covariance(points[...], anchors)
 
             @pl.when((m >= 0) & (m < PIECES))
             def _():
@@ -461,8 +468,8 @@
     dma = pltpu.SemaphoreType.DMA
     return pl.pallas_call(
         body,
-        out_shape=jax.ShapeDtypeStruct((TILE, B), F32),
-        in_specs=[pl.BlockSpec(memory_space=pltpu.VMEM), pl.BlockSpec(memory_space=pl.ANY)],
+        out_shape=pltpu.VMEM((TILE, B), F32),
+        in_specs=[pl.BlockSpec(memory_space=pl.ANY)] * 2,
         out_specs=pl.BlockSpec(memory_space=pltpu.VMEM),
         scratch_shapes=[
             pltpu.VMEM((2, ROWS, SLAB), F32),
@@ -480,6 +487,9 @@
             pltpu.VMEM((10 * TILE, TILE), F32),
             pltpu.VMEM((TILE, TILE), F32),
             pltpu.VMEM((TILE, B), F32),
+            pltpu.VMEM((FEAT, TILE), F32),
+            pltpu.VMEM((FEAT, B), F32),
+            dma((2,)),
             dma((2, 2)),
             dma((4, 4)),
             dma((PIECES, 4)),

time: 82.2 us -> 79.5 us (0.967)
  Pallas kernels: 80.2 us -> 78.5 us
  local copies, waits for them, and re-layouts: 1.67 us -> 0.71 us
    pallas_call x1, Pallas kernels: 80.2 us -> 78.5 us  [on_device(): pl.pallas_call(body, out_shape=pltpu.VMEM((TILE, B), F32), in_specs=[pl.B...]
    unnamed x1, local copies, waits for them, and re-layouts: 1.67 us -> 0.71 us
where the time goes in v3:
time: 79.5 us; the launch traced here: 79.2 us
  Pallas kernels  78.5 us (99%)
    pallas_call x1, Pallas kernels, on_device(): pl.pallas_call(body, out_shape=pltpu.VMEM((TILE, B), F32), in_specs=[pl.B...  78.5 us

profile of v3, /device:TPU:37, one launch (start us, length us, event | category | flops | bytes accessed | tf_op | source)
XLA Modules:
  0.0 79.2 jit_solution(5839922547362175615)
XLA Ops:
  0.0 78.5 %shard_map.28 = f32[128,512]{1,0:T(8,128)S(1)} custom-call(f32[136,1024]{1,0:T(8,128)} %feat_ref.1, f32[1024,4096]{1,0:T(8,128)} %factor_ref.1), custom_call_target="tpu_custom_call" | custom-call | tf_op jit(solution)/shard_map/pallas_call | solution.py:469
  78.5 0.7 copy.4

commit v4 on v3

--- a/solution.py
+++ b/solution.py
@@ -37,7 +37,7 @@
 
 
 def lag(depth):
-    return depth * 3 - 1
+    return depth * 7 // 2 - 1
 
 
 def pick(index, table):
@@ -319,6 +319,10 @@
         sums[...] = jnp.zeros_like(sums)
 
         def slot(s, carry):
+            @pl.when(s - last == PIECES)
+            def _():
+                send_parts(3, 0)
+
             for t in range(4):
                 item = s - lags[t]
 
@@ -363,10 +367,6 @@
                     load(s + 2).start()
 
             m = s - last
-
-            @pl.when(m == PIECES)
-            def _():
-                send_parts(3, 0)
 
             @pl.when(m == PIECES + 2)
             def _():

time: 79.5 us -> 78.9 us (level)
  no operation moved by 1% of the time
where the time goes in v4:
time: 78.9 us; the launch traced here: 78.6 us
  Pallas kernels  77.9 us (99%)
    pallas_call x1, Pallas kernels, on_device(): pl.pallas_call(body, out_shape=pltpu.VMEM((TILE, B), F32), in_specs=[pl.B...  77.9 us

profile of v4, /device:TPU:37, one launch (start us, length us, event | category | flops | bytes accessed | tf_op | source)
XLA Modules:
  0.0 78.6 jit_solution(32919173529070381)
XLA Ops:
  0.0 77.9 %shard_map.28 = f32[128,512]{1,0:T(8,128)S(1)} custom-call(f32[136,1024]{1,0:T(8,128)} %feat_ref.1, f32[1024,4096]{1,0:T(8,128)} %factor_ref.1), custom_call_target="tpu_custom_call" | custom-call | tf_op jit(solution)/shard_map/pallas_call | solution.py:469
  77.9 0.7 copy.4

commit v5 on v4

--- a/solution.py
+++ b/solution.py
@@ -37,7 +37,7 @@
 
 
 def lag(depth):
-    return depth * 7 // 2 - 1
+    return depth * 7 // 2 - 2
 
 
 def pick(index, table):
@@ -172,17 +172,18 @@
     def send_low(j, t, d):
         remote(low_at(j, t, core), low_at(j, t, core), low_send.at[t, d], low_recv.at[j, t], (near[d], col)).start()
 
-    def accumulate(slab, block, panel):
+    def accumulate(slab, block, panel, first=0, count=ROWS):
         panel_high, panel_low = panel
-        a = nt(high[slab], jnp.concatenate([panel_high, panel_low], 0))
-        b = nt(low[slab], panel_high)
-        sums[block] += a[:, :TILE] + a[:, TILE:] + b
+        at = pl.ds(first, count)
+        a = nt(high[slab, at, :], jnp.concatenate([panel_high, panel_low], 0))
+        b = nt(low[slab, at, :], panel_high)
+        sums[block, at, :] += a[:, :TILE] + a[:, TILE:] + b
 
     def owned(q, c):
         return pl.ds(pl.multiple_of((q * 2 + c) * TILE, TILE), TILE)
 
-    def send_pair(block, first):
-        for q in range(first, 4):
+    def send_pair(block, first, end=4):
+        for q in range(first, end):
             src = sums.at[block, owned(q, 1 - core), :]
             remote(src, pair.at[block, q], pair_send, pair_recv.at[block], (row, sibling)).start()
 
@@ -376,7 +377,14 @@
                 own_points.wait()
                 slab_kernel[...] = covariance(points[...], anchors)
 
-            @pl.when((m >= 0) & (m < PIECES))
+            @pl.when(m == PIECES - 1)
+            def _():
+                panel = two_parts(land[PIECES - 1])
+                for q in (0, 2):
+                    accumulate(SLABS - 1, 3, panel, q * 2 * TILE, ROWS // 2)
+                    send_pair(3, q, q + 2)
+
+            @pl.when((m >= 0) & (m < PIECES - 1))
             def _():
                 block, slab = m // SLABS, m % SLABS
                 accumulate(slab, block, two_parts(land[m]))
@@ -428,27 +436,19 @@
         solved.append(value)
         out_ref[:, j * TILE : (j + 1) * TILE] = value
 
-    for j in range(4):
+    for j in range(3):
         solve(j, rest(j))
+    remainder = rest(3)
 
     @pl.when(row != 0)
     def _():
         arrived(feat_land.at[:, :, pl.ds(0, B // 2)], share_send)
         arrived(lower.at[pl.ds(0, 5 * TILE), :], share_send)
         arrived(pair, pair_send)
-        arrived(parts.at[:, pl.ds(0, 3)], part_send)
 
     @pl.when(row == 0)
     def _():
         arrived(pair.at[:, pl.ds(0, 2)], pair_send)
-
-        @pl.when(pivot)
-        def _():
-            arrived(parts.at[:, pl.ds(0, 2)], part_send)
-
-        @pl.when(jnp.logical_not(pivot))
-        def _():
-            arrived(parts.at[:, 0], part_send)
 
     for t in range(4):
         for d in range(4):
@@ -462,6 +462,22 @@
     def _():
         for phase in range(2):
             arrived(gram_parts.at[pl.ds(0, 7)], gram_send.at[phase])
+
+    solve(3, remainder)
+
+    @pl.when(row != 0)
+    def _():
+        arrived(parts.at[:, pl.ds(0, 3)], part_send)
+
+    @pl.when(row == 0)
+    def _():
+        @pl.when(pivot)
+        def _():
+            arrived(parts.at[:, pl.ds(0, 2)], part_send)
+
+        @pl.when(jnp.logical_not(pivot))
+        def _():
+            arrived(parts.at[:, 0], part_send)
 
 
 def on_device(features, factor):

time: 78.9 us -> 79 us (level)
  no operation moved by 1% of the time
where the time goes in v5:
time: 79 us; the launch traced here: 78.7 us
  Pallas kernels  78 us (99%)
    pallas_call x1, Pallas kernels, on_device(): pl.pallas_call(body, out_shape=pltpu.VMEM((TILE, B), F32), in_specs=[pl.B...  78 us

profile of v5, /device:TPU:37, one launch (start us, length us, event | category | flops | bytes accessed | tf_op | source)
XLA Modules:
  0.0 78.7 jit_solution(2133211894371940568)
XLA Ops:
  0.0 78.0 %shard_map.28 = f32[128,512]{1,0:T(8,128)S(1)} custom-call(f32[136,1024]{1,0:T(8,128)} %feat_ref.1, f32[1024,4096]{1,0:T(8,128)} %factor_ref.1), custom_call_target="tpu_custom_call" | custom-call | tf_op jit(solution)/shard_map/pallas_call | solution.py:485
  78.0 0.7 copy.4
